TPU v7x, 512 devices: a whole 4x8x8 slice. The times are simulated.
512 devices in a mesh: flop: 4 (over x), turn: 16 (over y, core), river: 8 (over z).
Axes of the slice: x: 4, y: 8, z: 8, core: 2. Of those that a mesh axis runs over, the one named last changes fastest.
Arguments:
- regrets: float32 [4, 256, 1326], P('flop', ('turn', 'river')), may hold values from -6 to 6
- opp_reach: bfloat16 [4, 256, 1326], P('flop', ('turn', 'river')), may hold values from 0 to 1
- pot_size: int32 [4, 256], P('flop', ('turn', 'river')), may hold values from 1 to 8
- line_kind: int32 [4, 256], P('flop', ('turn', 'river')), may hold values from 0 to 2
- board_lines: int32 [4, 16, 16, 256], P('flop', 'turn', 'river'), may hold values from 0 to 255, as said below
- board_count: int32 [4, 16, 16], P('flop', 'turn', 'river'), may hold values from 64 to 256, as said below
- hand_ranks: int32 [4, 16, 16, 1326], P('flop', 'turn', 'river'), may hold values from 0 to 7461
- live_hands: int32 [4, 16, 16, 1326], P('flop', 'turn', 'river'), may hold values 0 or 1
Outputs:
- new_regrets: float32 [4, 256, 1326], P('flop', ('turn', 'river'))
- chance_values: float32 [128, 1326], P(('turn', 'river'))
Inputs may be any that keep to these rules, and one draw needn't show every extreme that they name: `board_lines`: each board lists 256 different lines of its flop; its first board_count slots hold the lines live on it, the other slots add nothing. `board_count`: in every flop one board has all 256 slots live and another only 64.
All inputs are finite; a program needn't handle non-finite values. No bound on the sum of `live_hands` on one device may be relied on, other than what follows from the above.
Results may differ from a plain program's by a relative error of at most 0.0003.
Values may be sent and summed in bfloat16 or wider, within the bound.
A program may use at most 64 MiB of HBM per device.

v0:
```python
import jax
import jax.numpy as jnp
import numpy as np
from jax import lax
from jax.sharding import PartitionSpec as P

CARDS = 52
ACTS = 2


floor_share = 0.1


def disjoint_table(card_count):
    card_first, card_second = np.triu_indices(card_count, 1)
    first_cards = jnp.asarray(card_first.astype(np.int32))
    second_cards = jnp.asarray(card_second.astype(np.int32))
    apart = (first_cards[:, None] != first_cards[None, :]) & (
        first_cards[:, None] != second_cards[None, :]
    )
    apart = (
        apart
        & (second_cards[:, None] != first_cards[None, :])
        & (second_cards[:, None] != second_cards[None, :])
    )
    return apart


def payoff_matrix(board_ranks, board_live, apart):
    both_live = apart & (board_live[:, None] > 0) & (board_live[None, :] > 0)
    fold_part = both_live.astype(jnp.float32)
    ordering = jnp.sign(board_ranks[None, :] - board_ranks[:, None]).astype(jnp.float32)
    return jnp.concatenate([fold_part * ordering, fold_part], axis=1).astype(jnp.bfloat16)


def on_device(
    regrets, opp_reach, pot_size, line_kind, board_lines, board_count, hand_ranks, live_hands
):
    hand_count = opp_reach.shape[2]
    boards_here = board_lines.shape[2]
    board_total = lax.axis_size("turn") * lax.axis_size("river") * boards_here
    pot_float = pot_size.astype(jnp.float32)
    show_coef = jnp.where(line_kind == 0, pot_float, 0.0)
    fold_coef = jnp.where(line_kind == 1, -pot_float, jnp.where(line_kind == 2, pot_float, 0.0))
    line_coef = jnp.stack([show_coef, fold_coef], axis=2).astype(jnp.bfloat16)
    reach_whole, coef_whole = (
        lax.all_gather(opp_reach, ("turn", "river"), axis=1, tiled=True),
        lax.all_gather(line_coef, ("turn", "river"), axis=1, tiled=True),
    )
    reach_whole = reach_whole[0]
    coef_whole = coef_whole[0]
    line_total = reach_whole.shape[0]
    slot_total = board_lines.shape[3]
    apart = disjoint_table(CARDS)
    chance_scale = 1.0 / (board_total * hand_count)
    line_table = jnp.zeros((line_total, hand_count), jnp.float32)
    for board_index in range(boards_here):
        slot_lines = board_lines[0, 0, board_index]
        live_count = board_count[0, 0, board_index]
        slot_reach = jnp.take(reach_whole, slot_lines, axis=0)
        slot_coef = jnp.take(coef_whole, slot_lines, axis=0).astype(jnp.float32)
        matrix = payoff_matrix(hand_ranks[0, 0, board_index], live_hands[0, 0, board_index], apart)

        def evaluate(
            first_row,
            row_count,
            slot_reach=slot_reach,
            slot_coef=slot_coef,
            matrix=matrix,
            live_count=live_count,
        ):
            products = jnp.dot(slot_reach, matrix, preferred_element_type=jnp.float32)
            slot_ids = first_row + jnp.arange(row_count, dtype=jnp.int32)
            keep_mask = (slot_ids < live_count).astype(jnp.float32)
            board_value = (
                slot_coef[:, 0:1] * products[:, :hand_count]
                + slot_coef[:, 1:2] * products[:, hand_count:]
            )
            return board_value * (chance_scale * keep_mask)[:, None]

        values = evaluate(0, slot_total)
        position = (
            jnp.full((line_total,), slot_total, jnp.int32)
            .at[slot_lines]
            .set(jnp.arange(slot_total, dtype=jnp.int32))
        )
        padded_values = jnp.concatenate([values, jnp.zeros((1, hand_count), jnp.float32)], axis=0)
        line_table = line_table + jnp.take(padded_values, position, axis=0)
    line_values = lax.psum_scatter(
        lax.slice_in_dim(
            line_table, 0, regrets.shape[1] * lax.axis_size(("turn", "river")), axis=0
        ),
        ("turn", "river"),
        scatter_dimension=0,
        tiled=True,
    )
    held_regret = regrets[0]
    group_total = held_regret.shape[0] // ACTS
    grouped = held_regret.reshape(group_total, ACTS, hand_count)
    worth_lines = line_values.reshape(group_total, ACTS, hand_count)
    positive = jnp.maximum(grouped, 0.0)
    strategy = (positive + floor_share) / (
        jnp.sum(positive, axis=1, keepdims=True) + ACTS * floor_share
    )
    node_values = jnp.sum(strategy * worth_lines, axis=1)
    updated = jnp.maximum(grouped + worth_lines - node_values[:, None, :], 0.0).reshape(
        held_regret.shape
    )
    chance_values = lax.psum(node_values, "flop") / lax.axis_size("flop")
    return (updated[None], chance_values)


def solution(mesh):
    placed = (
        P("flop", ("turn", "river"), None),
        P("flop", ("turn", "river"), None),
        P("flop", ("turn", "river")),
        P("flop", ("turn", "river")),
        P("flop", "turn", "river", None),
        P("flop", "turn", "river"),
        P("flop", "turn", "river", None),
        P("flop", "turn", "river", None),
    )
    return jax.shard_map(
        on_device,
        mesh=mesh,
        in_specs=placed,
        out_specs=(P("flop", ("turn", "river"), None), P(("turn", "river"), None)),
        check_vma=False,
    )
```

profile of v0, /device:TPU:24, one launch (start us, length us, event | category | flops | bytes accessed | tf_op | source)
XLA Modules:
  0.0 440.4 jit_solution(8097442302047093316)
XLA Ops:
  7.2 0.8 fusion.31
  8.0 0.8 compare_select_fusion.1
  8.8 0.7 copy.27
  9.5 94.9 %all_gather.7 = bf16[1,256,1326]{2,0,1:T(2,128)(2,1)S(1)} all-gather(bf16[1,2,1326]{2,0,1:T(2,128)(2,1)S(1)} %copy.27), channel_id=1, replica_groups=mesh['flop'=4,'turn'=16,'river'=8] {'turn','river'}, dimensions={1}, use_global_device_ids=true | all-gather | bytes 684216 | tf_op jit(solution)/shard_map/all_gather | solution.py:47
  104.7 67.3 %all_gather.6 = bf16[1,256,2]{2,0,1:T(2,128)(2,1)S(1)} all-gather(bf16[1,2,2]{2,0,1:T(2,128)(2,1)S(1)} %copy.24), channel_id=1, replica_groups=mesh['flop'=4,'turn'=16,'river'=8] {'turn','river'}, dimensions={1}, use_global_device_ids=true | all-gather | bytes 1032 | tf_op jit(solution)/shard_map/all_gather | solution.py:48
  172.2 1.3 gather_fusion.1
  173.6 0.9 gather_fusion
  174.5 2.1 gather_fusion.4
  176.6 0.9 gather_fusion.3
  177.5 1.4 scatter_custom_fusion
  178.9 1.4 scatter_custom_fusion.1
  180.8 0.6 fusion.32
  181.3 0.6 compare_select_fusion.7
  182.0 5.2 %convert_convert_fusion.1 = (bf16[1326,1326]{1,0:T(8,128)(2,1)S(1)}, bf16[1326,1326]{1,0:T(8,128)(2,1)}) fusion(pred[1326]{0:T(1024)(128)(4,1)S(1)} %get-tuple-element.11, s32[1326]{0:T(1024)S(1)} %copy-done.3, s32[1326]{0:T(1024)S(1)} %copy-done.2, pred[1326]{0:T(1024)(128)(4,1)S(1)} %get-tuple-element.12), kind=kLoop, calls=%fused_computation.10 | loop fusion | flops 26374140 | bytes 7046364 | tf_op jit(solution)/shard_map/convert.3
  187.2 8.7 %select_convert_fusion.1 = (bf16[1326,1326]{1,0:T(8,128)(2,1)S(1)}, bf16[1326,1326]{1,0:T(8,128)(2,1)}) fusion(s32[1326]{0:T(1024)S(1)} %get-tuple-element.9, pred[1326]{0:T(1024)(128)(4,1)S(1)} %get-tuple-element.11, s32[1326]{0:T(1024)S(1)} %copy-done.3, s32[1326]{0:T(1024)S(1)} %copy-done.2, s32[1326]{0:T(1024)S(1)} %get-tuple-element.10, ...), kind=kLoop, calls=%fused_computation.11 | loop fusion | flops 36923796 | bytes 7056972 | tf_op jit(solution)/shard_map/convert.2
  196.0 5.3 %fusion = f32[256,2652]{0,1:T(8,128)S(1)} fusion(bf16[1326,1326]{1,0:T(8,128)(2,1)S(1)} %get-tuple-element.15, bf16[1326,1326]{1,0:T(8,128)(2,1)S(1)} %get-tuple-element.13, bf16[256,1326]{1,0:T(8,128)(2,1)S(1)} %gather_fusion.1, pred[256]{0:T(512)(128)(4,1)S(1)} %compare_and_fusion.4), kind=kOutput, calls=%fused_computation.15 | convolution fusion | flops 1814880256 | bytes 10427920 | tf_op jit(solution)/shard_map/dot_general | solution.py:72
  201.3 0.3 fusion.11
  201.6 0.4 copy.36
  202.3 0.7 compare_select_fusion.6
  203.0 8.6 %fusion.4 = f32[256,2652]{0,1:T(8,128)S(1)} fusion(bf16[1326,1326]{1,0:T(8,128)(2,1)} %get-tuple-element.16, bf16[1326,1326]{1,0:T(8,128)(2,1)} %get-tuple-element.14, bf16[256,1326]{1,0:T(8,128)(2,1)} %gather_fusion.4, pred[256]{0:T(512)(128)(4,1)S(1)} %compare_and_fusion.2), kind=kOutput, calls=%fused_computation.19 | convolution fusion | flops 1814880256 | bytes 10427920 | tf_op jit(solution)/shard_map/dot_general | solution.py:72
  211.6 0.3 fusion.9
  211.8 1.6 copy.37
  213.5 1.3 copy-done.1
  214.9 2.3 gather_fusion.2
  217.2 2.3 gather_fusion.5
  219.5 2.7 select_add_fusion
  222.2 1.3 dynamic-slice
  224.2 196.0 %all-reduce.5.cloned.1.call-done = f32[256,1326]{1,0:T(8,128)} async-done(((f32[256,1326]{1,0:T(8,128)}), f32[256,1326]{1,0:T(8,128)}) %all-reduce.5.cloned.1.call-update) | async-done | bytes 1357840
  420.2 0.8 fusion.18
  421.1 10.5 %psum.7 = f32[1,1326]{1,0:T(1,128)S(1)} all-reduce(f32[1,1326]{1,0:T(1,128)S(1)} %reduce_sum.22), channel_id=1, replica_groups=mesh['flop'=4,'turn'=16,'river'=8] {'flop'}, use_global_device_ids=true, to_apply=%region_5.9 | all-reduce | flops 1326 | bytes 10608 | tf_op jit(solution)/shard_map/psum | solution.py:109
  431.6 0.6 broadcast_multiply_fusion
  432.2 1.4 subtract_maximum_fusion
  (51 shorter events, 1.5 us)
Async XLA Ops:
  7.2 97.4 %copy-start.9 = (s32[1,2]{1,0:T(1,128)S(1)}, s32[1,2]{1,0:T(1,128)}, u32[]{:S(2)}) copy-start(s32[1,2]{1,0:T(1,128)} %param.18) | copy-start | bytes 28
  7.2 97.4 %copy-start.8 = (s32[1,2]{1,0:T(1,128)S(1)}, s32[1,2]{1,0:T(1,128)}, u32[]{:S(2)}) copy-start(s32[1,2]{1,0:T(1,128)} %param.19) | copy-start | bytes 28
  7.2 413.0 %all-reduce.5.cloned.1.call-start = ((), (), s32[]{:S(2)}) async-start(), calls=%async_computation | async-start | bytes 2883584
  174.4 5.9 %copy-start.6 = (s32[1,1,2,1326]{3,2,1,0:T(2,128)S(1)}, s32[1,1,2,1326]{3,2,1,0:T(2,128)}, u32[]{:S(2)}) copy-start(s32[1,1,2,1326]{3,2,1,0:T(2,128)} %param.23) | copy-start | bytes 31828
  174.4 6.0 %copy-start.5 = (s32[1,1,2,1326]{3,2,1,0:T(2,128)S(1)}, s32[1,1,2,1326]{3,2,1,0:T(2,128)}, u32[]{:S(2)}) copy-start(s32[1,1,2,1326]{3,2,1,0:T(2,128)} %param.22) | copy-start | bytes 31828
  174.4 6.3 %copy-start.7 = (s32[1,1,2]{2,1,0:T(1,128)S(1)}, s32[1,1,2]{2,1,0:T(1,128)}, u32[]{:S(2)}) copy-start(s32[1,1,2]{2,1,0:T(1,128)} %param.21) | copy-start | bytes 28
  174.5 7.5 %copy-start.2 = (s32[1326]{0:T(1024)S(1)}, s32[1326]{0:T(1024)}, u32[]{:S(2)}) copy-start(s32[1326]{0:T(1024)} %constant.44.clone) | copy-start | bytes 15916
  174.5 7.5 %copy-start.3 = (s32[1326]{0:T(1024)S(1)}, s32[1326]{0:T(1024)}, u32[]{:S(2)}) copy-start(s32[1326]{0:T(1024)} %constant.45.clone) | copy-start | bytes 15916
  213.4 1.4 copy-start.1
  217.2 2.3 copy-start
  219.5 4.7 %copy-start.4 = (f32[1,2,1326]{2,1,0:T(2,128)S(1)}, f32[1,2,1326]{2,1,0:T(2,128)}, u32[]{:S(2)}) copy-start(f32[1,2,1326]{2,1,0:T(2,128)} %param.16) | copy-start | bytes 31828
Sparse Core Ops, SparseCore 0:
  222.3 197.8 all-reduce.4
where the time goes:
time: 441 us; the launch traced here: 440 us
  waiting for transfers between devices  196 us (44%)
  blocking collectives  173 us (39%)
  other arithmetic  22.5 us (5%)
  local copies, waits for them, and re-layouts  20.2 us (5%)
  between operations  15 us (3%)
  matrix products  13.9 us (3%)
    unnamed x2, waiting for transfers between devices  196 us
    all_gather x1, blocking collectives, on_device(): lax.all_gather(opp_reach, ('turn', 'river'), axis=1, tiled=True)  94.9 us
    all_gather x1, blocking collectives, on_device(): lax.all_gather(line_coef, ('turn', 'river'), axis=1, tiled=True)  67.3 us
    another operation x2, other arithmetic  14 us
    dot_general x2, matrix products, evaluate(): products = jnp.dot(slot_reach, matrix, preferred_element_type=jnp.float32)  13.9 us
    psum x1, blocking collectives, on_device(): chance_values = lax.psum(node_values, 'flop') / lax.axis_size('flop')  10.5 us
  transfers between devices with their start and end apart: 1, of which 1 were waited for; matrix products, arithmetic and copies ran while one was open for 0% of the time, Pallas kernels for 0%

commit v1 on v0

v1 whole, which is shorter than its diff:
```python
import functools

import jax
import jax.numpy as jnp
import numpy as np
from jax import lax
from jax.experimental import pallas as pl
from jax.experimental.pallas import tpu as pltpu
from jax.sharding import PartitionSpec as P

CARDS = 52
H = 1326
LANES = 128
HP = 1408
TILES = HP // LANES
SPLIT = 768
BOARDS = 256
FLOOR = 0.1
N = 8
MESH = pl.DeviceIdType.MESH
BF16 = jnp.bfloat16
F32 = jnp.float32

CHUNKS = ((0, 0, 256), (1, 768, 256), (0, 256, 256), (1, 1024, 256), (0, 512, 256), (1, 1280, 128))


def card_tables():
    first, second = np.triu_indices(CARDS, 1)
    hands = np.arange(H)
    left = np.zeros((HP, LANES), np.float32)
    left[hands, first] = -1.0
    left[hands, second] = -1.0
    left[:, CARDS] = 1.0
    right = np.zeros((LANES, HP), np.float32)
    right[first, hands] = 1.0
    right[second, hands] = 1.0
    right[CARDS, :] = 1.0
    return left.astype(BF16), right.astype(BF16)


def kernel(
    regrets, reach, pot, kind, lines, count, ranks, live, cards_left, cards_right,
    new_regrets, chance,
    apart, show, held, board, col_hi, col_lo, row_hi, row_lo, row_lv, keep, lhs_show, lhs_fold,
    part, recv1, mid, recv2, node,
    sem_board, ag_send, ag_recv, rs1_send, rs1_recv, rs2_send, rs2_recv, fl_send, fl_recv,
):
    f = lax.axis_index("flop")
    t = lax.axis_index("turn")
    z = lax.axis_index("river")
    y = t // 2
    c = t % 2

    def z_peer(d):
        return lax.rem(z + d, N)

    def y_peer(d):
        return lax.rem(y + d, N)

    def on_z(d):
        return (f, t, z_peer(d))

    def on_y(d):
        return (f, 2 * y_peer(d) + c, z)

    other_core = (f, 2 * y + (1 - c), z)

    barrier = pltpu.get_barrier_semaphore()
    for d in range(1, N):
        pl.semaphore_signal(barrier, inc=1, device_id=on_z(d), device_id_type=MESH)
        pl.semaphore_signal(barrier, inc=1, device_id=on_y(d), device_id_type=MESH)
    pl.semaphore_signal(barrier, inc=1, device_id=other_core, device_id_type=MESH)
    for d in range(1, 4):
        pl.semaphore_signal(barrier, inc=1, device_id=(lax.rem(f + d, 4), t, z), device_id_type=MESH)

    held[y, z] = jnp.zeros((2, HP), BF16)
    held[y, z, :, 0:H] = reach[...]
    row_id = lax.broadcasted_iota(jnp.int32, (2, LANES), 0)
    lane_id = lax.broadcasted_iota(jnp.int32, (2, LANES), 1)
    flag0 = jnp.where(kind[0, 0] == 0, 1.0, 0.0).astype(F32)
    flag1 = jnp.where(kind[0, 1] == 0, 1.0, 0.0).astype(F32)
    flags = jnp.where(lane_id == H - (TILES - 1) * LANES, jnp.where(row_id == 0, flag0, flag1), 0.0)
    tail = held[y, z, :, (TILES - 1) * LANES : HP].astype(F32)
    held[y, z, :, (TILES - 1) * LANES : HP] = (tail + flags).astype(BF16)

    board[0] = jnp.zeros((8, HP), F32)
    rank_high = (ranks[...] >> 7) << 7
    board[0, 0:2, 0:H] = rank_high.astype(F32)
    board[0, 2:4, 0:H] = (ranks[...] - rank_high).astype(F32)
    board[0, 4:6, 0:H] = live[...].astype(F32)
    slot_row = lax.broadcasted_iota(jnp.int32, (2, 256), 0)
    slot_id = lax.broadcasted_iota(jnp.int32, (2, 256), 1)
    limit = jnp.where(slot_row == 0, count[0], count[1])
    board[0, 6:8, 0:256] = jnp.where(slot_id < limit, lines[...], -1).astype(F32)

    pl.semaphore_wait(barrier, 18)

    def remote(src, dst, send, recv, device):
        copy = pltpu.make_async_remote_copy(
            src_ref=src, dst_ref=dst, send_sem=send, recv_sem=recv, device_id=device, device_id_type=MESH
        )
        copy.start()
        return copy

    board_copy = remote(board.at[0], board.at[1], sem_board.at[0], sem_board.at[1], other_core)
    ag1 = []
    for d in range(1, N):
        own = held.at[y, z, :, 0:SPLIT]
        ag1.append(remote(own, own, ag_send.at[0, d], ag_recv.at[0, d], on_z(d)))
        own = held.at[y, z, :, SPLIT:HP]
        ag1.append(remote(own, own, ag_send.at[1, d], ag_recv.at[1, d], on_y(d)))

    def spread(i, carry):
        rows = pl.ds(pl.multiple_of(i * 128, 128), 128)
        for first, width in ((0, 512), (512, 512), (1024, 384)):
            cols = slice(first, first + width)
            free = jnp.dot(cards_left[rows, :], cards_right[:, cols], preferred_element_type=F32)
            apart[rows, cols] = jnp.maximum(free, 0.0).astype(BF16)
        return carry

    lax.fori_loop(0, TILES, spread, 0)

    def prepare(s):
        for k in range(2):
            b = 2 * s + k
            for j in range(TILES):
                cols = slice(j * LANES, (j + 1) * LANES)
                col_hi[b, cols, :] = jnp.broadcast_to(board[s, k : k + 1, cols], (LANES, LANES)).T.astype(BF16)
                col_lo[b, cols, :] = jnp.broadcast_to(board[s, 2 + k : 3 + k, cols], (LANES, LANES)).T.astype(BF16)
            row_hi[b] = jnp.broadcast_to(board[s, k : k + 1, :], (16, HP)).astype(BF16)
            row_lo[b] = jnp.broadcast_to(board[s, 2 + k : 3 + k, :], (16, HP)).astype(BF16)
            row_lv[b] = jnp.broadcast_to(board[s, 4 + k : 5 + k, :], (16, HP)).astype(BF16)
            row = lax.broadcasted_iota(jnp.int32, (128, 256), 0)
            line_a = 32 * ((row // 2) % 8) + 16 * c + 2 * (row // 16) + row % 2
            line_b = 32 * (row // 16) + 16 * c + row % 16
            slots = jnp.broadcast_to(board[s, 6 + k : 7 + k, 0:256], (128, 256))
            for o, line in enumerate((line_a, line_b)):
                hit = jnp.where(slots == line.astype(F32), 1.0, 0.0)
                keep[o, b] = jnp.broadcast_to(jnp.sum(hit, axis=1, keepdims=True), (128, LANES)).astype(BF16)

    def generate(s):
        def step(i, carry):
            rows = pl.ds(pl.multiple_of(i * 16, 16), 16)
            for k in range(2):
                b = 2 * s + k
                hi = col_hi[b, rows, :]
                lo = col_lo[b, rows, :]
                for j in range(TILES):
                    cols = slice(j * LANES, (j + 1) * LANES)
                    bound = row_lv[b, :, cols]
                    gap = ((row_hi[b, :, cols] - hi) + (row_lo[b, :, cols] - lo)) * apart[rows, cols]
                    show[b, rows, cols] = jnp.maximum(jnp.minimum(gap, bound), -bound)
            return carry

        lax.fori_loop(0, HP // 16, step, 0)

    prepare(0)
    generate(0)

    for copy in ag1:
        copy.wait_recv()
    ag2 = []
    for d in range(1, N):
        row = held.at[y, :, :, 0:SPLIT]
        ag2.append(remote(row, row, ag_send.at[2, d], ag_recv.at[2, d], on_y(d)))
        column = held.at[:, z, :, SPLIT:HP]
        ag2.append(remote(column, column, ag_send.at[3, d], ag_recv.at[3, d], on_z(d)))

    board_copy.wait_recv()
    prepare(1)
    generate(1)

    for copy in ag2:
        copy.wait_recv()

    tail_lane = lax.broadcasted_iota(jnp.int32, (16, LANES), 1)

    def build(i, carry):
        for o in range(2):
            block = held[:, i] if o == 0 else held[i]
            block = block.reshape(16, HP)
            rows = pl.ds(pl.multiple_of(i * 16, 16), 16)
            tail = block[:, (TILES - 1) * LANES : HP].astype(F32)
            tail = jnp.where(tail_lane == H - (TILES - 1) * LANES, tail, 0.0)
            flag = jnp.broadcast_to(jnp.sum(tail, axis=1, keepdims=True), (16, LANES)).astype(BF16)
            for b in range(4):
                kept = keep[o, b, rows, :]
                fold_rows = pl.ds(pl.multiple_of(b * 128 + i * 16, 16), 16)
                for j in range(TILES):
                    cols = slice(j * LANES, (j + 1) * LANES)
                    masked = block[:, cols] * kept * row_lv[b, :, cols]
                    shown = masked * flag
                    lhs_show[o, b, rows, cols] = shown
                    lhs_fold[o, fold_rows, cols] = masked - shown
        return carry

    lax.fori_loop(0, N, build, 0)

    rs1 = []
    for n, (o, first, width) in enumerate(CHUNKS):
        cols = slice(first, first + width)
        folded = jnp.dot(lhs_fold[o], apart[:, cols], preferred_element_type=F32)
        total = jnp.dot(lhs_show[o, 0], show[0, :, cols], preferred_element_type=F32)
        for b in range(1, 4):
            total += jnp.dot(lhs_show[o, b], show[b, :, cols], preferred_element_type=F32)
        for b in range(4):
            total += folded[b * 128 : (b + 1) * 128] * board[b // 2, 4 + b % 2 : 5 + b % 2, cols]
        part[n, :, 0:width] = total
        copies = []
        for d in range(1, N):
            target = z_peer(d) if o == 0 else y_peer(d)
            src = part.at[n, pl.ds(pl.multiple_of(target * 16, 16), 16), 0:width]
            copies.append(
                remote(src, recv1.at[n, d, :, 0:width], rs1_send.at[n, d], rs1_recv.at[n, d], on_z(d) if o == 0 else on_y(d))
            )
        rs1.append(copies)

    rs2 = []
    for n, (o, first, width) in enumerate(CHUNKS):
        mine = z if o == 0 else y
        total = part[n, pl.ds(pl.multiple_of(mine * 16, 16), 16), 0:width]
        for d in range(1, N):
            rs1[n][d - 1].wait_recv()
        for d in range(1, N):
            total += recv1[n, d, :, 0:width]
        for q in range(N):
            mid[q, :, first : first + width] = total[2 * q : 2 * q + 2]
        if n >= len(CHUNKS) - 2:
            cols = slice(0, SPLIT) if o == 0 else slice(SPLIT, HP)
            for d in range(1, N):
                target = y_peer(d) if o == 0 else z_peer(d)
                rs2.append(
                    remote(
                        mid.at[target, :, cols], recv2.at[d, :, cols], rs2_send.at[o, d], rs2_recv.at[o, d],
                        on_y(d) if o == 0 else on_z(d),
                    )
                )
    for copy in rs2:
        copy.wait_recv()
    value_a = mid[y, :, 0:SPLIT]
    value_b = mid[z, :, SPLIT:H]
    for d in range(1, N):
        value_a += recv2[d, :, 0:SPLIT]
        value_b += recv2[d, :, SPLIT:H]
    row_id = lax.broadcasted_iota(jnp.int32, (2, LANES), 0)
    pots = [pot[0, a].astype(F32) for a in range(2)]
    coefs = [jnp.where(kind[0, a] == 1, -pots[a], pots[a]) * (1.0 / (BOARDS * H)) for a in range(2)]
    coef = jnp.where(row_id == 0, coefs[0], coefs[1])[:, 0:1]
    for first, last, value in ((0, SPLIT, value_a), (SPLIT, H, value_b)):
        worth = value * coef
        held_regret = regrets[:, first:last]
        positive = jnp.maximum(held_regret, 0.0)
        strategy = (positive + FLOOR) / (jnp.sum(positive, axis=0, keepdims=True) + 2 * FLOOR)
        decision = jnp.sum(strategy * worth, axis=0, keepdims=True)
        new_regrets[:, first:last] = jnp.maximum(held_regret + worth - decision, 0.0)
        node[f, :, first:last] = decision

    flops = []
    for d in range(1, 4):
        own = node.at[f]
        flops.append(remote(own, own, fl_send.at[d], fl_recv.at[d], (lax.rem(f + d, 4), t, z)))
    for copy in flops:
        copy.wait_recv()
    chance[...] = ((node[0] + node[1]) + (node[2] + node[3])) * 0.25

    board_copy.wait_send()
    for copy in ag1 + ag2 + rs2 + flops:
        copy.wait_send()
    for copies in rs1:
        for copy in copies:
            copy.wait_send()


def on_device(regrets, opp_reach, pot_size, line_kind, board_lines, board_count, hand_ranks, live_hands):
    vmem = pl.BlockSpec(memory_space=pltpu.VMEM)
    smem = pl.BlockSpec(memory_space=pltpu.SMEM)
    dma = pltpu.SemaphoreType.DMA
    left, right = card_tables()
    updated, chance = pl.pallas_call(
        kernel,
        out_shape=(jax.ShapeDtypeStruct((2, H), F32), jax.ShapeDtypeStruct((1, H), F32)),
        in_specs=[vmem, vmem, smem, smem, vmem, smem, vmem, vmem, vmem, vmem],
        out_specs=(vmem, vmem),
        scratch_shapes=[
            pltpu.VMEM((HP, HP), BF16),
            pltpu.VMEM((4, HP, HP), BF16),
            pltpu.VMEM((N, N, 2, HP), BF16),
            pltpu.VMEM((2, 8, HP), F32),
            pltpu.VMEM((4, HP, LANES), BF16),
            pltpu.VMEM((4, HP, LANES), BF16),
            pltpu.VMEM((4, 16, HP), BF16),
            pltpu.VMEM((4, 16, HP), BF16),
            pltpu.VMEM((4, 16, HP), BF16),
            pltpu.VMEM((2, 4, 128, LANES), BF16),
            pltpu.VMEM((2, 4, 128, HP), BF16),
            pltpu.VMEM((2, 512, HP), BF16),
            pltpu.VMEM((6, 128, 256), F32),
            pltpu.VMEM((6, N, 16, 256), F32),
            pltpu.VMEM((N, 2, HP), F32),
            pltpu.VMEM((N, 2, HP), F32),
            pltpu.VMEM((4, 1, H), F32),
            dma((2,)),
            dma((4, N)),
            dma((4, N)),
            dma((6, N)),
            dma((6, N)),
            dma((2, N)),
            dma((2, N)),
            dma((4,)),
            dma((4,)),
        ],
        compiler_params=pltpu.CompilerParams(
            collective_id=0, has_side_effects=True, vmem_limit_bytes=48 * 1024 * 1024
        ),
    )(
        regrets[0], opp_reach[0], pot_size, line_kind, board_lines[0, 0], board_count[0, 0],
        hand_ranks[0, 0], live_hands[0, 0], jnp.asarray(left), jnp.asarray(right),
    )
    return updated[None], chance


def solution(mesh):
    lines = ("turn", "river")
    placed = (
        P("flop", lines, None),
        P("flop", lines, None),
        P("flop", lines),
        P("flop", lines),
        P("flop", "turn", "river", None),
        P("flop", "turn", "river"),
        P("flop", "turn", "river", None),
        P("flop", "turn", "river", None),
    )
    return jax.shard_map(
        on_device,
        mesh=mesh,
        in_specs=placed,
        out_specs=(P("flop", lines, None), P(lines, None)),
        check_vma=False,
    )
```

time: 441 us -> 68 us (0.15)
  the two profiles are of different devices: /device:TPU:24 before, /device:TPU:2 now
where the time goes in v1:
time: 68 us; the launch traced here: 67.6 us
  Pallas kernels  58.3 us (86%)
  local copies, waits for them, and re-layouts  8.6 us (13%)
    pallas_call x1, Pallas kernels, on_device(): pl.pallas_call(kernel, out_shape=(jax.ShapeDtypeStruct((2, H), F32), jax....  58.3 us
    unnamed x22, local copies, waits for them, and re-layouts  8.6 us

profile of v1, /device:TPU:2, one launch (start us, length us, event | category | flops | bytes accessed | tf_op | source)
XLA Modules:
  0.0 67.6 jit_solution(9133461875079257069)
XLA Ops:
  0.6 0.0 copy-start.2
  0.6 0.7 %copy-done.2 = f32[1,2,1326]{2,1,0:T(2,128)S(1)} copy-done((f32[1,2,1326]{2,1,0:T(2,128)S(1)}, f32[1,2,1326]{2,1,0:T(2,128)}, u32[]{:S(2)}) %copy-start.2) | copy-done | bytes 10632
  1.3 0.0 copy-start
  1.3 1.0 %copy-done = bf16[128,1408]{1,0:T(8,128)(2,1)S(1)} copy-done((bf16[128,1408]{1,0:T(8,128)(2,1)S(1)}, bf16[128,1408]{1,0:T(8,128)(2,1)}, u32[]{:S(2)}) %copy-start) | copy-done | bytes 360472
  2.3 0.0 copy-start.1
  2.3 1.0 %copy-done.1 = bf16[1408,128]{1,0:T(8,128)(2,1)S(1)} copy-done((bf16[1408,128]{1,0:T(8,128)(2,1)S(1)}, bf16[1408,128]{1,0:T(8,128)(2,1)}, u32[]{:S(2)}) %copy-start.1) | copy-done | bytes 360472
  3.3 0.0 copy-start.3
  3.3 0.7 %copy-done.3 = s32[1,1,2,1326]{3,2,1,0:T(2,128)S(1)} copy-done((s32[1,1,2,1326]{3,2,1,0:T(2,128)S(1)}, s32[1,1,2,1326]{3,2,1,0:T(2,128)}, u32[]{:S(2)}) %copy-start.3) | copy-done | bytes 10632
  4.0 0.0 copy-start.4
  4.0 0.7 %copy-done.4 = s32[1,1,2,1326]{3,2,1,0:T(2,128)S(1)} copy-done((s32[1,1,2,1326]{3,2,1,0:T(2,128)S(1)}, s32[1,1,2,1326]{3,2,1,0:T(2,128)}, u32[]{:S(2)}) %copy-start.4) | copy-done | bytes 10632
  4.7 0.0 copy-start.5
  4.7 0.7 %copy-done.5 = bf16[1,2,1326]{2,1,0:T(2,128)(2,1)S(1)} copy-done((bf16[1,2,1326]{2,1,0:T(2,128)(2,1)S(1)}, bf16[1,2,1326]{2,1,0:T(2,128)(2,1)}, u32[]{:S(2)}) %copy-start.5) | copy-done | bytes 5328
  5.4 0.0 copy-start.6
  5.4 0.7 %copy-done.6 = s32[1,1,2,256]{3,2,1,0:T(2,128)S(1)} copy-done((s32[1,1,2,256]{3,2,1,0:T(2,128)S(1)}, s32[1,1,2,256]{3,2,1,0:T(2,128)}, u32[]{:S(2)}) %copy-start.6) | copy-done | bytes 2072
  6.1 0.0 copy-start.7
  6.1 0.7 copy-done.7
  6.7 0.0 copy-start.8
  6.7 0.7 copy-done.8
  7.4 0.0 copy-start.9
  7.4 0.7 copy-done.9
  8.1 58.3 %shard_map.113 = (f32[2,1326]{1,0:T(2,128)S(1)}, f32[1,1326]{1,0:T(1,128)S(1)}) custom-call(f32[2,1326]{1,0:T(2,128)S(1)} %bitcast.8, bf16[2,1326]{1,0:T(2,128)(2,1)S(1)} %bitcast.11, s32[1,2]{1,0:T(1,128)S(1)} %copy-done.7, s32[1,2]{1,0:T(1,128)S(1)} %copy-done.8, s32[2,256]{1,0:T(2,128)S(1)} %bitcast.12, s32[2]{0:T(128)S(1)} %bitcast.13, ...), custom_call_target="tpu_custom_call" | custom-call | tf_op jit(solution)/shard_map/pallas_call | solution.py:279
  66.4 0.6 copy.14
  67.0 0.6 copy.15
Async XLA Ops:
  0.6 0.7 %copy-start.2 = (f32[1,2,1326]{2,1,0:T(2,128)S(1)}, f32[1,2,1326]{2,1,0:T(2,128)}, u32[]{:S(2)}) copy-start(f32[1,2,1326]{2,1,0:T(2,128)} %param.10) | copy-start | bytes 31828
  1.3 1.0 %copy-start = (bf16[128,1408]{1,0:T(8,128)(2,1)S(1)}, bf16[128,1408]{1,0:T(8,128)(2,1)}, u32[]{:S(2)}) copy-start(bf16[128,1408]{1,0:T(8,128)(2,1)} %constant.5.clone.cards_right) | copy-start | bytes 1081348
  2.3 1.0 %copy-start.1 = (bf16[1408,128]{1,0:T(8,128)(2,1)S(1)}, bf16[1408,128]{1,0:T(8,128)(2,1)}, u32[]{:S(2)}) copy-start(bf16[1408,128]{1,0:T(8,128)(2,1)} %constant.4.clone.cards_left) | copy-start | bytes 1081348
  3.3 0.7 %copy-start.3 = (s32[1,1,2,1326]{3,2,1,0:T(2,128)S(1)}, s32[1,1,2,1326]{3,2,1,0:T(2,128)}, u32[]{:S(2)}) copy-start(s32[1,1,2,1326]{3,2,1,0:T(2,128)} %param.16) | copy-start | bytes 31828
  4.0 0.7 %copy-start.4 = (s32[1,1,2,1326]{3,2,1,0:T(2,128)S(1)}, s32[1,1,2,1326]{3,2,1,0:T(2,128)}, u32[]{:S(2)}) copy-start(s32[1,1,2,1326]{3,2,1,0:T(2,128)} %param.17) | copy-start | bytes 31828
  4.7 0.7 %copy-start.5 = (bf16[1,2,1326]{2,1,0:T(2,128)(2,1)S(1)}, bf16[1,2,1326]{2,1,0:T(2,128)(2,1)}, u32[]{:S(2)}) copy-start(bf16[1,2,1326]{2,1,0:T(2,128)(2,1)} %param.11) | copy-start | bytes 15916
  5.4 0.7 %copy-start.6 = (s32[1,1,2,256]{3,2,1,0:T(2,128)S(1)}, s32[1,1,2,256]{3,2,1,0:T(2,128)}, u32[]{:S(2)}) copy-start(s32[1,1,2,256]{3,2,1,0:T(2,128)} %param.14) | copy-start | bytes 6148
  6.1 0.7 copy-start.7
  6.7 0.7 copy-start.8
  7.4 0.7 copy-start.9

commit v2 on v1

v2 whole, which is shorter than its diff:
```python
import functools

import jax
import jax.numpy as jnp
import numpy as np
from jax import lax
from jax.experimental import pallas as pl
from jax.experimental.pallas import tpu as pltpu
from jax.sharding import PartitionSpec as P

CARDS = 52
H = 1326
LANES = 128
HP = 1408
TILES = HP // LANES
SPLIT = 768
TAIL = HP - LANES
FLAG_LANE = H - TAIL
BOARDS = 256
FLOOR = 0.1
N = 8
PARTS = (0, 128, 192)
MESH = pl.DeviceIdType.MESH
BF16 = jnp.bfloat16
F32 = jnp.float32

CHUNKS = ((0, 0, 256), (1, 768, 256), (0, 256, 256), (1, 1024, 256), (0, 512, 256), (1, 1280, 128))


def card_tables():
    first, second = np.triu_indices(CARDS, 1)
    hands = np.arange(H)
    left = np.zeros((HP, 256), np.float32)
    right = np.zeros((256, HP), np.float32)
    for start in PARTS:
        left[hands, start + first] = -1.0
        left[hands, start + second] = -1.0
        left[:, start + CARDS] = 1.0
        right[start + first, hands] = 1.0
        right[start + second, hands] = 1.0
        right[start + CARDS, :] = 1.0
    return left.astype(BF16), right.astype(BF16)


def kernel(*refs):
    sources, (new_regrets, chance), inputs, rest = refs[0:10], refs[10:12], refs[12:22], refs[22:]
    regrets, reach, pot, kind, lines, count, ranks, live, cards_left, cards_right = inputs
    (
        apart, minus_apart, show, line_a, line_b, rows_a, rows_b, board, col_hi, col_lo, row_hi, row_lo, row_lv,
        keep, raw, lhs_show, lhs_fold, sums,
        part, recv1, mid, recv2, node,
        sem_in, sem_board, ag_send, ag_recv, rs1_send, rs1_recv, rs2_send, rs2_recv, fl_send, fl_recv,
    ) = rest
    f = lax.axis_index("flop")
    t = lax.axis_index("turn")
    z = lax.axis_index("river")
    y = t // 2
    c = t % 2

    def z_peer(d):
        return lax.rem(z + d, N)

    def y_peer(d):
        return lax.rem(y + d, N)

    def on_z(d):
        return (f, t, z_peer(d))

    def on_y(d):
        return (f, 2 * y_peer(d) + c, z)

    other_core = (f, 2 * y + (1 - c), z)

    loads = [pltpu.make_async_copy(sources[k], inputs[k], sem_in.at[k]) for k in range(10)]
    for load in loads:
        load.start()

    barrier = pltpu.get_barrier_semaphore()
    for d in range(1, N):
        pl.semaphore_signal(barrier, inc=1, device_id=on_z(d), device_id_type=MESH)
        pl.semaphore_signal(barrier, inc=1, device_id=on_y(d), device_id_type=MESH)
    pl.semaphore_signal(barrier, inc=1, device_id=other_core, device_id_type=MESH)
    for d in range(1, 4):
        pl.semaphore_signal(barrier, inc=1, device_id=(lax.rem(f + d, 4), t, z), device_id_type=MESH)

    for load in loads:
        load.wait()

    row_id = lax.broadcasted_iota(jnp.int32, (2, LANES), 0)
    lane_id = lax.broadcasted_iota(jnp.int32, (2, LANES), 1)
    flag0 = jnp.where(kind[0, 0] == 0, 1.0, 0.0).astype(F32)
    flag1 = jnp.where(kind[0, 1] == 0, 1.0, 0.0).astype(F32)
    flags = jnp.where(lane_id == FLAG_LANE, jnp.where(row_id == 0, flag0, flag1), 0.0)
    line_a[z] = reach[:, 0:SPLIT]
    line_b[y] = jnp.zeros((2, HP - SPLIT), BF16)
    line_b[y, :, 0 : H - SPLIT] = reach[:, SPLIT:H]
    tail = line_b[y, :, TAIL - SPLIT : HP - SPLIT].astype(F32)
    line_b[y, :, TAIL - SPLIT : HP - SPLIT] = (tail + flags).astype(BF16)

    board[0] = jnp.zeros((8, HP), F32)
    rank_high = (ranks[...] >> 7) << 7
    board[0, 0:2, 0:H] = rank_high.astype(F32)
    board[0, 2:4, 0:H] = (ranks[...] - rank_high).astype(F32)
    board[0, 4:6, 0:H] = live[...].astype(F32)
    slot_row = lax.broadcasted_iota(jnp.int32, (2, 256), 0)
    slot_id = lax.broadcasted_iota(jnp.int32, (2, 256), 1)
    limit = jnp.where(slot_row == 0, count[0, 0], count[0, 1])
    board[0, 6:8, 0:256] = jnp.where(slot_id < limit, lines[...], -1).astype(F32)

    def spread(i, carry):
        rows = pl.ds(pl.multiple_of(i * 128, 128), 128)
        for first, width in ((0, 512), (512, 512), (1024, 384)):
            cols = slice(first, first + width)
            free = jnp.dot(cards_left[rows, 0:128], cards_right[0:128, cols], preferred_element_type=F32)
            free = jnp.maximum(free, 0.0).astype(BF16)
            apart[rows, cols] = free
            minus_apart[rows, cols] = -free
        return carry

    lax.fori_loop(0, TILES, spread, 0)

    def prepare(s):
        for k in range(2):
            b = 2 * s + k
            for j in range(TILES):
                cols = slice(j * LANES, (j + 1) * LANES)
                col_hi[b, cols, :] = jnp.broadcast_to(board[s, k : k + 1, cols], (LANES, LANES)).T.astype(BF16)
                col_lo[b, cols, :] = jnp.broadcast_to(board[s, 2 + k : 3 + k, cols], (LANES, LANES)).T.astype(BF16)
            row_hi[b] = jnp.broadcast_to(board[s, k : k + 1, :], (16, HP)).astype(BF16)
            row_lo[b] = jnp.broadcast_to(board[s, 2 + k : 3 + k, :], (16, HP)).astype(BF16)
            row_lv[b] = jnp.broadcast_to(board[s, 4 + k : 5 + k, :], (16, HP)).astype(BF16)
            row = lax.broadcasted_iota(jnp.int32, (128, 256), 0)
            in_a = 32 * ((row // 2) % 8) + 16 * c + 2 * (row // 16) + row % 2
            in_b = 32 * (row // 16) + 16 * c + row % 16
            slots = jnp.broadcast_to(board[s, 6 + k : 7 + k, 0:256], (128, 256))
            for o, line in enumerate((in_a, in_b)):
                hit = jnp.where(slots == line.astype(F32), 1.0, 0.0)
                keep[o, b] = jnp.broadcast_to(jnp.sum(hit, axis=1, keepdims=True), (128, LANES)).astype(BF16)

    def generate(s):
        def step(i, carry):
            rows = pl.ds(pl.multiple_of(i * 64, 64), 64)
            for j in range(TILES):
                cols = slice(j * LANES, (j + 1) * LANES)
                bound = apart[rows, cols]
                minus_bound = minus_apart[rows, cols]
                for k in range(2):
                    b = 2 * s + k
                    high = jnp.concatenate([row_hi[b, :, cols]] * 4, axis=0) - col_hi[b, rows, :]
                    low = jnp.concatenate([row_lo[b, :, cols]] * 4, axis=0) - col_lo[b, rows, :]
                    show[b, rows, cols] = jnp.maximum(jnp.minimum(high + low, bound), minus_bound)
            return carry

        lax.fori_loop(0, HP // 64, step, 0)

    pl.semaphore_wait(barrier, 18)

    def remote(src, dst, send, recv, device):
        copy = pltpu.make_async_remote_copy(
            src_ref=src, dst_ref=dst, send_sem=send, recv_sem=recv, device_id=device, device_id_type=MESH
        )
        copy.start()
        return copy

    board_copy = remote(board.at[0], board.at[1], sem_board.at[0], sem_board.at[1], other_core)
    ag1a, ag1b = [], []
    for d in range(1, N):
        ag1a.append(remote(line_a.at[z], line_a.at[z], ag_send.at[0, d], ag_recv.at[0, d], on_z(d)))
        ag1b.append(remote(line_b.at[y], line_b.at[y], ag_send.at[1, d], ag_recv.at[1, d], on_y(d)))

    prepare(0)
    ag2 = []
    for copy in ag1a:
        copy.wait_recv()
    rows_a[y] = line_a[...].reshape(16, SPLIT)
    for d in range(1, N):
        ag2.append(remote(rows_a.at[y], rows_a.at[y], ag_send.at[2, d], ag_recv.at[2, d], on_y(d)))
    for copy in ag1b:
        copy.wait_recv()
    rows_b[z] = line_b[...].reshape(16, HP - SPLIT)
    for d in range(1, N):
        ag2.append(remote(rows_b.at[z], rows_b.at[z], ag_send.at[3, d], ag_recv.at[3, d], on_z(d)))

    generate(0)
    board_copy.wait_recv()
    prepare(1)
    generate(1)

    for copy in ag2:
        copy.wait_recv()

    out_row = lax.broadcasted_iota(jnp.int32, (128, 128), 0)
    in_row = lax.broadcasted_iota(jnp.int32, (128, 128), 1)
    swapped = 16 * ((out_row // 2) % 8) + 2 * (out_row // 16) + out_row % 2
    swap = jnp.where(in_row == swapped, 1.0, 0.0).astype(BF16)
    own_a = rows_a[...].reshape(128, SPLIT)
    own_b = rows_b[...].reshape(128, HP - SPLIT)
    raw[1, :, 0:SPLIT] = own_a
    raw[0, :, SPLIT:HP] = own_b
    raw[0, :, 0:SPLIT] = jnp.dot(swap, own_a, preferred_element_type=F32).astype(BF16)
    raw[1, :, SPLIT:HP] = jnp.dot(swap, own_b, preferred_element_type=F32).astype(BF16)

    tail_lane = lax.broadcasted_iota(jnp.int32, (16, LANES), 1)

    def build(i, carry):
        rows = pl.ds(pl.multiple_of(i * 16, 16), 16)
        for o in range(2):
            tail = jnp.where(tail_lane == FLAG_LANE, raw[o, rows, TAIL:HP].astype(F32), 0.0)
            flag = jnp.broadcast_to(jnp.sum(tail, axis=1, keepdims=True), (16, LANES)).astype(BF16)
            for b in range(4):
                kept = keep[o, b, rows, :]
                shown = kept * flag
                folded = kept - shown
                fold_rows = pl.ds(pl.multiple_of(b * 128 + i * 16, 16), 16)
                for j in range(TILES):
                    cols = slice(j * LANES, (j + 1) * LANES)
                    masked = raw[o, rows, cols] * row_lv[b, :, cols]
                    lhs_show[o, b, rows, cols] = masked * shown
                    lhs_fold[o, fold_rows, cols] = masked * folded
        return carry

    lax.fori_loop(0, N, build, 0)

    part_lane = lax.broadcasted_iota(jnp.int32, (128, 256), 1)

    def card_sums(o):
        for b in range(4):
            rows = slice(b * 128, (b + 1) * 128)
            whole = jnp.dot(lhs_fold[o, rows, :], cards_left[...], preferred_element_type=F32)
            top = whole.astype(BF16).astype(F32)
            rest = whole - top
            middle = rest.astype(BF16).astype(F32)
            split = jnp.where(part_lane < PARTS[1], top, jnp.where(part_lane < PARTS[2], middle, rest - middle))
            sums[o, rows, :] = split.astype(BF16)

    rs1 = []
    for n, (o, first, width) in enumerate(CHUNKS):
        cols = slice(first, first + width)
        if n < 2:
            card_sums(o)
        folded = jnp.dot(sums[o], cards_right[:, cols], preferred_element_type=F32)
        total = jnp.zeros((128, width), F32)
        for b in range(4):
            shown = jnp.dot(lhs_show[o, b], show[b, :, cols], preferred_element_type=F32)
            own = lhs_fold[o, b * 128 : (b + 1) * 128, cols].astype(F32)
            total += ((folded[b * 128 : (b + 1) * 128] + own) + shown) * board[b // 2, 4 + b % 2 : 5 + b % 2, cols]
        part[n, :, 0:width] = total
        copies = []
        for d in range(1, N):
            target = z_peer(d) if o == 0 else y_peer(d)
            src = part.at[n, pl.ds(pl.multiple_of(target * 16, 16), 16), 0:width]
            copies.append(
                remote(src, recv1.at[n, d, :, 0:width], rs1_send.at[n, d], rs1_recv.at[n, d], on_z(d) if o == 0 else on_y(d))
            )
        rs1.append(copies)

    rs2 = []
    for n, (o, first, width) in enumerate(CHUNKS):
        mine = z if o == 0 else y
        total = part[n, pl.ds(pl.multiple_of(mine * 16, 16), 16), 0:width]
        for d in range(1, N):
            rs1[n][d - 1].wait_recv()
        for d in range(1, N):
            total += recv1[n, d, :, 0:width]
        for q in range(N):
            mid[q, :, first : first + width] = total[2 * q : 2 * q + 2]
        if n >= len(CHUNKS) - 2:
            cols = slice(0, SPLIT) if o == 0 else slice(SPLIT, HP)
            for d in range(1, N):
                target = y_peer(d) if o == 0 else z_peer(d)
                rs2.append(
                    remote(
                        mid.at[target, :, cols], recv2.at[d, :, cols], rs2_send.at[o, d], rs2_recv.at[o, d],
                        on_y(d) if o == 0 else on_z(d),
                    )
                )
    for copy in rs2:
        copy.wait_recv()
    value_a = mid[y, :, 0:SPLIT]
    value_b = mid[z, :, SPLIT:H]
    for d in range(1, N):
        value_a += recv2[d, :, 0:SPLIT]
        value_b += recv2[d, :, SPLIT:H]
    row_id = lax.broadcasted_iota(jnp.int32, (2, LANES), 0)
    pots = [pot[0, a].astype(F32) for a in range(2)]
    coefs = [jnp.where(kind[0, a] == 1, -pots[a], pots[a]) * (1.0 / (BOARDS * H)) for a in range(2)]
    coef = jnp.where(row_id == 0, coefs[0], coefs[1])[:, 0:1]
    for first, last, value in ((0, SPLIT, value_a), (SPLIT, H, value_b)):
        worth = value * coef
        held_regret = regrets[:, first:last]
        positive = jnp.maximum(held_regret, 0.0)
        strategy = (positive + FLOOR) / (jnp.sum(positive, axis=0, keepdims=True) + 2 * FLOOR)
        decision = jnp.sum(strategy * worth, axis=0, keepdims=True)
        new_regrets[:, first:last] = jnp.maximum(held_regret + worth - decision, 0.0)
        node[f, :, first:last] = decision

    flops = []
    for d in range(1, 4):
        own = node.at[f]
        flops.append(remote(own, own, fl_send.at[d], fl_recv.at[d], (lax.rem(f + d, 4), t, z)))
    for copy in flops:
        copy.wait_recv()
    chance[...] = ((node[0] + node[1]) + (node[2] + node[3])) * 0.25

    board_copy.wait_send()
    for copy in ag1a + ag1b + ag2 + rs2 + flops:
        copy.wait_send()
    for copies in rs1:
        for copy in copies:
            copy.wait_send()


def on_device(regrets, opp_reach, pot_size, line_kind, board_lines, board_count, hand_ranks, live_hands):
    vmem = pl.BlockSpec(memory_space=pltpu.VMEM)
    hbm = pl.BlockSpec(memory_space=pltpu.HBM)
    dma = pltpu.SemaphoreType.DMA
    left, right = card_tables()
    updated, chance = pl.pallas_call(
        kernel,
        out_shape=(jax.ShapeDtypeStruct((2, H), F32), jax.ShapeDtypeStruct((1, H), F32)),
        in_specs=[hbm] * 10,
        out_specs=(vmem, vmem),
        scratch_shapes=[
            pltpu.VMEM((2, H), F32),
            pltpu.VMEM((2, H), BF16),
            pltpu.SMEM((1, 2), jnp.int32),
            pltpu.SMEM((1, 2), jnp.int32),
            pltpu.VMEM((2, 256), jnp.int32),
            pltpu.SMEM((1, 2), jnp.int32),
            pltpu.VMEM((2, H), jnp.int32),
            pltpu.VMEM((2, H), jnp.int32),
            pltpu.VMEM((HP, 256), BF16),
            pltpu.VMEM((256, HP), BF16),
            pltpu.VMEM((HP, HP), BF16),
            pltpu.VMEM((HP, HP), BF16),
            pltpu.VMEM((4, HP, HP), BF16),
            pltpu.VMEM((N, 2, SPLIT), BF16),
            pltpu.VMEM((N, 2, HP - SPLIT), BF16),
            pltpu.VMEM((N, 16, SPLIT), BF16),
            pltpu.VMEM((N, 16, HP - SPLIT), BF16),
            pltpu.VMEM((2, 8, HP), F32),
            pltpu.VMEM((4, HP, LANES), BF16),
            pltpu.VMEM((4, HP, LANES), BF16),
            pltpu.VMEM((4, 16, HP), BF16),
            pltpu.VMEM((4, 16, HP), BF16),
            pltpu.VMEM((4, 16, HP), BF16),
            pltpu.VMEM((2, 4, 128, LANES), BF16),
            pltpu.VMEM((2, 128, HP), BF16),
            pltpu.VMEM((2, 4, 128, HP), BF16),
            pltpu.VMEM((2, 512, HP), BF16),
            pltpu.VMEM((2, 512, 256), BF16),
            pltpu.VMEM((6, 128, 256), F32),
            pltpu.VMEM((6, N, 16, 256), F32),
            pltpu.VMEM((N, 2, HP), F32),
            pltpu.VMEM((N, 2, HP), F32),
            pltpu.VMEM((4, 1, H), F32),
            dma((10,)),
            dma((2,)),
            dma((4, N)),
            dma((4, N)),
            dma((6, N)),
            dma((6, N)),
            dma((2, N)),
            dma((2, N)),
            dma((4,)),
            dma((4,)),
        ],
        compiler_params=pltpu.CompilerParams(
            collective_id=0, has_side_effects=True, vmem_limit_bytes=63 * 1024 * 1024
        ),
    )(
        regrets[0], opp_reach[0], pot_size, line_kind, board_lines[0, 0], board_count[0],
        hand_ranks[0, 0], live_hands[0, 0], jnp.asarray(left), jnp.asarray(right),
    )
    return updated[None], chance


def solution(mesh):
    lines = ("turn", "river")
    placed = (
        P("flop", lines, None),
        P("flop", lines, None),
        P("flop", lines),
        P("flop", lines),
        P("flop", "turn", "river", None),
        P("flop", "turn", "river"),
        P("flop", "turn", "river", None),
        P("flop", "turn", "river", None),
    )
    return jax.shard_map(
        on_device,
        mesh=mesh,
        in_specs=placed,
        out_specs=(P("flop", lines, None), P(lines, None)),
        check_vma=False,
    )
```

time: 68 us -> 54.8 us (0.81)
  the two profiles are of different devices: /device:TPU:2 before, /device:TPU:64 now
where the time goes in v2:
time: 54.8 us; the launch traced here: 54.6 us
  Pallas kernels  52 us (95%)
  local copies, waits for them, and re-layouts  1.91 us (3%)
  between operations  0.65 us (1%)
    pallas_call x1, Pallas kernels, on_device(): pl.pallas_call(kernel, out_shape=(jax.ShapeDtypeStruct((2, H), F32), jax....  52 us
    unnamed x4, local copies, waits for them, and re-layouts  1.91 us

profile of v2, /device:TPU:64, one launch (start us, length us, event | category | flops | bytes accessed | tf_op | source)
XLA Modules:
  0.0 54.6 jit_solution(16870928543237505764)
XLA Ops:
  0.6 52.0 %shard_map.113 = (f32[2,1326]{1,0:T(2,128)}, f32[1,1326]{1,0:T(1,128)}) custom-call(f32[2,1326]{1,0:T(2,128)} %bitcast.8, bf16[2,1326]{1,0:T(2,128)(2,1)} %bitcast.11, s32[1,2]{1,0:T(1,128)} %refs_2_.1, s32[1,2]{1,0:T(1,128)} %refs_3_.1, s32[2,256]{1,0:T(2,128)} %bitcast.12, s32[1,2]{1,0:T(1,128)} %bitcast.13, s32[2,1326]{1,0:T(2,128)} %bitcast.9, ...), custom_call_target="tpu_custom_call" | custom-call | tf_op jit(solution)/shard_map/pallas_call | solution.py:318
  52.6 0.0 copy-start
  52.6 1.3 %copy.14 = f32[1,2,1326]{2,1,0:T(2,128)} copy(f32[1,2,1326]{2,1,0:T(2,128)} %bitcast.7) | data formatting | bytes 21216
  54.0 0.0 copy-done
  54.0 0.6 %copy.15 = f32[1,1326]{1,0:T(1,128)} copy(f32[1,1326]{1,0:T(1,128)S(1)} %copy-done) | data formatting | bytes 10608
Async XLA Ops:
  52.6 1.3 %copy-start = (f32[1,1326]{1,0:T(1,128)S(1)}, f32[1,1326]{1,0:T(1,128)}, u32[]{:S(2)}) copy-start(f32[1,1326]{1,0:T(1,128)} %get-tuple-element.9) | copy-start | bytes 15916

commit v3 on v2

--- a/solution.py
+++ b/solution.py
@@ -47,9 +47,9 @@
     regrets, reach, pot, kind, lines, count, ranks, live, cards_left, cards_right = inputs
     (
         apart, minus_apart, show, line_a, line_b, rows_a, rows_b, board, col_hi, col_lo, row_hi, row_lo, row_lv,
-        keep, raw, lhs_show, lhs_fold, sums,
-        part, recv1, mid, recv2, node,
-        sem_in, sem_board, ag_send, ag_recv, rs1_send, rs1_recv, rs2_send, rs2_recv, fl_send, fl_recv,
+        keep, raw, shows, lhs, sums,
+        part_a, part_b, recv_a, recv_b, mid, recv2, node,
+        sem_in, sem_board, ag_send, ag_recv, rs1_send, rs1_recv, rs2_send, rs2_recv, fl_sems,
     ) = rest
     f = lax.axis_index("flop")
     t = lax.axis_index("turn")
@@ -130,12 +130,10 @@
             row_lo[b] = jnp.broadcast_to(board[s, 2 + k : 3 + k, :], (16, HP)).astype(BF16)
             row_lv[b] = jnp.broadcast_to(board[s, 4 + k : 5 + k, :], (16, HP)).astype(BF16)
             row = lax.broadcasted_iota(jnp.int32, (128, 256), 0)
-            in_a = 32 * ((row // 2) % 8) + 16 * c + 2 * (row // 16) + row % 2
-            in_b = 32 * (row // 16) + 16 * c + row % 16
+            line = 32 * (row // 16) + 16 * c + row % 16
             slots = jnp.broadcast_to(board[s, 6 + k : 7 + k, 0:256], (128, 256))
-            for o, line in enumerate((in_a, in_b)):
-                hit = jnp.where(slots == line.astype(F32), 1.0, 0.0)
-                keep[o, b] = jnp.broadcast_to(jnp.sum(hit, axis=1, keepdims=True), (128, LANES)).astype(BF16)
+            hit = jnp.where(slots == line.astype(F32), 1.0, 0.0)
+            keep[b] = jnp.broadcast_to(jnp.sum(hit, axis=1, keepdims=True), (128, LANES)).astype(BF16)
 
     def generate(s):
         def step(i, carry):
@@ -160,122 +158,113 @@
             src_ref=src, dst_ref=dst, send_sem=send, recv_sem=recv, device_id=device, device_id_type=MESH
         )
         copy.start()
-        return copy
-
-    board_copy = remote(board.at[0], board.at[1], sem_board.at[0], sem_board.at[1], other_core)
-    ag1a, ag1b = [], []
-    for d in range(1, N):
-        ag1a.append(remote(line_a.at[z], line_a.at[z], ag_send.at[0, d], ag_recv.at[0, d], on_z(d)))
-        ag1b.append(remote(line_b.at[y], line_b.at[y], ag_send.at[1, d], ag_recv.at[1, d], on_y(d)))
+
+    def arrived(sem, ref):
+        pltpu.make_async_copy(ref, ref, sem).wait()
+
+    remote(board.at[0], board.at[1], sem_board.at[0], sem_board.at[1], other_core)
+    for d in range(1, N):
+        remote(line_a.at[z], line_a.at[z], ag_send.at[0], ag_recv.at[0], on_z(d))
+        remote(line_b.at[y], line_b.at[y], ag_send.at[1], ag_recv.at[1], on_y(d))
 
     prepare(0)
-    ag2 = []
-    for copy in ag1a:
-        copy.wait_recv()
+    arrived(ag_recv.at[0], line_a.at[0 : N - 1])
     rows_a[y] = line_a[...].reshape(16, SPLIT)
     for d in range(1, N):
-        ag2.append(remote(rows_a.at[y], rows_a.at[y], ag_send.at[2, d], ag_recv.at[2, d], on_y(d)))
-    for copy in ag1b:
-        copy.wait_recv()
+        remote(rows_a.at[y], rows_a.at[y], ag_send.at[2], ag_recv.at[2], on_y(d))
+    arrived(ag_recv.at[1], line_b.at[0 : N - 1])
     rows_b[z] = line_b[...].reshape(16, HP - SPLIT)
     for d in range(1, N):
-        ag2.append(remote(rows_b.at[z], rows_b.at[z], ag_send.at[3, d], ag_recv.at[3, d], on_z(d)))
+        remote(rows_b.at[z], rows_b.at[z], ag_send.at[3], ag_recv.at[3], on_z(d))
 
     generate(0)
-    board_copy.wait_recv()
+    arrived(sem_board.at[1], board.at[1])
     prepare(1)
     generate(1)
 
-    for copy in ag2:
-        copy.wait_recv()
+    arrived(ag_recv.at[2], rows_a.at[0 : N - 1])
+    arrived(ag_recv.at[3], rows_b.at[0 : N - 1])
 
     out_row = lax.broadcasted_iota(jnp.int32, (128, 128), 0)
     in_row = lax.broadcasted_iota(jnp.int32, (128, 128), 1)
     swapped = 16 * ((out_row // 2) % 8) + 2 * (out_row // 16) + out_row % 2
     swap = jnp.where(in_row == swapped, 1.0, 0.0).astype(BF16)
-    own_a = rows_a[...].reshape(128, SPLIT)
-    own_b = rows_b[...].reshape(128, HP - SPLIT)
-    raw[1, :, 0:SPLIT] = own_a
-    raw[0, :, SPLIT:HP] = own_b
-    raw[0, :, 0:SPLIT] = jnp.dot(swap, own_a, preferred_element_type=F32).astype(BF16)
-    raw[1, :, SPLIT:HP] = jnp.dot(swap, own_b, preferred_element_type=F32).astype(BF16)
-
-    tail_lane = lax.broadcasted_iota(jnp.int32, (16, LANES), 1)
+    raw[:, 0:SPLIT] = rows_a[...].reshape(128, SPLIT)
+    raw[:, SPLIT:HP] = jnp.dot(swap, rows_b[...].reshape(128, HP - SPLIT), preferred_element_type=F32).astype(BF16)
+    tail_lane = lax.broadcasted_iota(jnp.int32, (128, LANES), 1)
+    tail = jnp.where(tail_lane == FLAG_LANE, raw[:, TAIL:HP].astype(F32), 0.0)
+    shows[...] = jnp.broadcast_to(jnp.sum(tail, axis=1, keepdims=True), (128, 256))
 
     def build(i, carry):
         rows = pl.ds(pl.multiple_of(i * 16, 16), 16)
-        for o in range(2):
-            tail = jnp.where(tail_lane == FLAG_LANE, raw[o, rows, TAIL:HP].astype(F32), 0.0)
-            flag = jnp.broadcast_to(jnp.sum(tail, axis=1, keepdims=True), (16, LANES)).astype(BF16)
-            for b in range(4):
-                kept = keep[o, b, rows, :]
-                shown = kept * flag
-                folded = kept - shown
-                fold_rows = pl.ds(pl.multiple_of(b * 128 + i * 16, 16), 16)
-                for j in range(TILES):
-                    cols = slice(j * LANES, (j + 1) * LANES)
-                    masked = raw[o, rows, cols] * row_lv[b, :, cols]
-                    lhs_show[o, b, rows, cols] = masked * shown
-                    lhs_fold[o, fold_rows, cols] = masked * folded
+        for b in range(4):
+            kept = keep[b, rows, :]
+            for j in range(TILES):
+                cols = slice(j * LANES, (j + 1) * LANES)
+                lhs[b, rows, cols] = raw[rows, cols] * kept * row_lv[b, :, cols]
         return carry
 
     lax.fori_loop(0, N, build, 0)
 
     part_lane = lax.broadcasted_iota(jnp.int32, (128, 256), 1)
 
-    def card_sums(o):
-        for b in range(4):
-            rows = slice(b * 128, (b + 1) * 128)
-            whole = jnp.dot(lhs_fold[o, rows, :], cards_left[...], preferred_element_type=F32)
-            top = whole.astype(BF16).astype(F32)
-            rest = whole - top
-            middle = rest.astype(BF16).astype(F32)
-            split = jnp.where(part_lane < PARTS[1], top, jnp.where(part_lane < PARTS[2], middle, rest - middle))
-            sums[o, rows, :] = split.astype(BF16)
-
-    rs1 = []
+    for b in range(4):
+        whole = jnp.dot(lhs[b], cards_left[...], preferred_element_type=F32)
+        top = whole.astype(BF16).astype(F32)
+        rest = whole - top
+        middle = rest.astype(BF16).astype(F32)
+        split = jnp.where(part_lane < PARTS[1], top, jnp.where(part_lane < PARTS[2], middle, rest - middle))
+        sums[b * 128 : (b + 1) * 128, :] = split.astype(BF16)
+
     for n, (o, first, width) in enumerate(CHUNKS):
         cols = slice(first, first + width)
-        if n < 2:
-            card_sums(o)
-        folded = jnp.dot(sums[o], cards_right[:, cols], preferred_element_type=F32)
+        m = n // 2
+        folded = jnp.dot(sums[...], cards_right[:, cols], preferred_element_type=F32)
+        is_show = shows[:, 0:width] > 0.5
         total = jnp.zeros((128, width), F32)
         for b in range(4):
-            shown = jnp.dot(lhs_show[o, b], show[b, :, cols], preferred_element_type=F32)
-            own = lhs_fold[o, b * 128 : (b + 1) * 128, cols].astype(F32)
-            total += ((folded[b * 128 : (b + 1) * 128] + own) + shown) * board[b // 2, 4 + b % 2 : 5 + b % 2, cols]
-        part[n, :, 0:width] = total
-        copies = []
+            shown = jnp.dot(lhs[b], show[b, :, cols], preferred_element_type=F32)
+            fold = folded[b * 128 : (b + 1) * 128] + lhs[b, :, cols].astype(F32)
+            total += jnp.where(is_show, shown, fold) * board[b // 2, 4 + b % 2 : 5 + b % 2, cols]
+        if o == 0:
+            part_a[m] = total.reshape(N, N, 2, width)
+        else:
+            part_b[m, :, 0:width] = total
         for d in range(1, N):
-            target = z_peer(d) if o == 0 else y_peer(d)
-            src = part.at[n, pl.ds(pl.multiple_of(target * 16, 16), 16), 0:width]
-            copies.append(
-                remote(src, recv1.at[n, d, :, 0:width], rs1_send.at[n, d], rs1_recv.at[n, d], on_z(d) if o == 0 else on_y(d))
-            )
-        rs1.append(copies)
-
-    rs2 = []
+            if o == 0:
+                src, dst, device = part_a.at[m, :, z_peer(d)], recv_a.at[m, d], on_z(d)
+            else:
+                src = part_b.at[m, pl.ds(pl.multiple_of(y_peer(d) * 16, 16), 16), 0:width]
+                dst, device = recv_b.at[m, d, :, 0:width], on_y(d)
+            remote(src, dst, rs1_send.at[n], rs1_recv.at[n], device)
+
+    def landed(n):
+        o, first, width = CHUNKS[n]
+        return recv_a.at[n // 2, 1:N] if o == 0 else recv_b.at[n // 2, 1:N, :, 0:width]
+
+    halves = (slice(0, SPLIT), slice(SPLIT, HP))
     for n, (o, first, width) in enumerate(CHUNKS):
-        mine = z if o == 0 else y
-        total = part[n, pl.ds(pl.multiple_of(mine * 16, 16), 16), 0:width]
-        for d in range(1, N):
-            rs1[n][d - 1].wait_recv()
-        for d in range(1, N):
-            total += recv1[n, d, :, 0:width]
-        for q in range(N):
-            mid[q, :, first : first + width] = total[2 * q : 2 * q + 2]
+        cols = slice(first, first + width)
+        m = n // 2
+        arrived(rs1_recv.at[n], landed(n))
+        if o == 0:
+            total = part_a[m, :, z]
+            for d in range(1, N):
+                total += recv_a[m, d]
+            mid[:, :, cols] = total
+        else:
+            total = part_b[m, pl.ds(pl.multiple_of(y * 16, 16), 16), 0:width]
+            for d in range(1, N):
+                total += recv_b[m, d, :, 0:width]
+            for q in range(N):
+                mid[q, :, cols] = total[2 * q : 2 * q + 2]
         if n >= len(CHUNKS) - 2:
-            cols = slice(0, SPLIT) if o == 0 else slice(SPLIT, HP)
+            whole = halves[o]
             for d in range(1, N):
-                target = y_peer(d) if o == 0 else z_peer(d)
-                rs2.append(
-                    remote(
-                        mid.at[target, :, cols], recv2.at[d, :, cols], rs2_send.at[o, d], rs2_recv.at[o, d],
-                        on_y(d) if o == 0 else on_z(d),
-                    )
-                )
-    for copy in rs2:
-        copy.wait_recv()
+                target, device = (y_peer(d), on_y(d)) if o == 0 else (z_peer(d), on_z(d))
+                remote(mid.at[target, :, whole], recv2.at[d, :, whole], rs2_send.at[o], rs2_recv.at[o], device)
+    arrived(rs2_recv.at[0], recv2.at[1:N, :, halves[0]])
+    arrived(rs2_recv.at[1], recv2.at[1:N, :, halves[1]])
     value_a = mid[y, :, 0:SPLIT]
     value_b = mid[z, :, SPLIT:H]
     for d in range(1, N):
@@ -294,20 +283,21 @@
         new_regrets[:, first:last] = jnp.maximum(held_regret + worth - decision, 0.0)
         node[f, :, first:last] = decision
 
-    flops = []
     for d in range(1, 4):
-        own = node.at[f]
-        flops.append(remote(own, own, fl_send.at[d], fl_recv.at[d], (lax.rem(f + d, 4), t, z)))
-    for copy in flops:
-        copy.wait_recv()
+        remote(node.at[f], node.at[f], fl_sems.at[0], fl_sems.at[1], (lax.rem(f + d, 4), t, z))
+    arrived(fl_sems.at[1], node.at[0:3])
     chance[...] = ((node[0] + node[1]) + (node[2] + node[3])) * 0.25
 
-    board_copy.wait_send()
-    for copy in ag1a + ag1b + ag2 + rs2 + flops:
-        copy.wait_send()
-    for copies in rs1:
-        for copy in copies:
-            copy.wait_send()
+    arrived(sem_board.at[0], board.at[0])
+    arrived(ag_send.at[0], line_a.at[0 : N - 1])
+    arrived(ag_send.at[1], line_b.at[0 : N - 1])
+    arrived(ag_send.at[2], rows_a.at[0 : N - 1])
+    arrived(ag_send.at[3], rows_b.at[0 : N - 1])
+    for n in range(len(CHUNKS)):
+        arrived(rs1_send.at[n], landed(n))
+    for o in range(2):
+        arrived(rs2_send.at[o], recv2.at[1:N, :, halves[o]])
+    arrived(fl_sems.at[0], node.at[0:3])
 
 
 def on_device(regrets, opp_reach, pot_size, line_kind, board_lines, board_count, hand_ranks, live_hands):
@@ -344,26 +334,27 @@
             pltpu.VMEM((4, 16, HP), BF16),
             pltpu.VMEM((4, 16, HP), BF16),
             pltpu.VMEM((4, 16, HP), BF16),
-            pltpu.VMEM((2, 4, 128, LANES), BF16),
-            pltpu.VMEM((2, 128, HP), BF16),
-            pltpu.VMEM((2, 4, 128, HP), BF16),
-            pltpu.VMEM((2, 512, HP), BF16),
-            pltpu.VMEM((2, 512, 256), BF16),
-            pltpu.VMEM((6, 128, 256), F32),
-            pltpu.VMEM((6, N, 16, 256), F32),
+            pltpu.VMEM((4, 128, LANES), BF16),
+            pltpu.VMEM((128, HP), BF16),
+            pltpu.VMEM((128, 256), F32),
+            pltpu.VMEM((4, 128, HP), BF16),
+            pltpu.VMEM((512, 256), BF16),
+            pltpu.VMEM((3, N, N, 2, 256), F32),
+            pltpu.VMEM((3, 128, 256), F32),
+            pltpu.VMEM((3, N, N, 2, 256), F32),
+            pltpu.VMEM((3, N, 16, 256), F32),
             pltpu.VMEM((N, 2, HP), F32),
             pltpu.VMEM((N, 2, HP), F32),
             pltpu.VMEM((4, 1, H), F32),
             dma((10,)),
             dma((2,)),
-            dma((4, N)),
-            dma((4, N)),
-            dma((6, N)),
-            dma((6, N)),
-            dma((2, N)),
-            dma((2, N)),
             dma((4,)),
             dma((4,)),
+            dma((6,)),
+            dma((6,)),
+            dma((2,)),
+            dma((2,)),
+            dma((2,)),
         ],
         compiler_params=pltpu.CompilerParams(
             collective_id=0, has_side_effects=True, vmem_limit_bytes=63 * 1024 * 1024

time: 54.8 us -> 50.6 us (0.923)
  the two profiles are of different devices: /device:TPU:64 before, /device:TPU:2 now
where the time goes in v3:
time: 50.6 us; the launch traced here: 50.4 us
  Pallas kernels  47.8 us (94%)
  local copies, waits for them, and re-layouts  1.91 us (4%)
  between operations  0.65 us (1%)
    pallas_call x1, Pallas kernels, on_device(): pl.pallas_call(kernel, out_shape=(jax.ShapeDtypeStruct((2, H), F32), jax....  47.8 us
    unnamed x4, local copies, waits for them, and re-layouts  1.91 us

profile of v3, /device:TPU:2, one launch (start us, length us, event | category | flops | bytes accessed | tf_op | source)
XLA Modules:
  0.0 50.4 jit_solution(512120767949930557)
XLA Ops:
  0.6 47.8 %shard_map.113 = (f32[2,1326]{1,0:T(2,128)}, f32[1,1326]{1,0:T(1,128)}) custom-call(f32[2,1326]{1,0:T(2,128)} %bitcast.8, bf16[2,1326]{1,0:T(2,128)(2,1)} %bitcast.11, s32[1,2]{1,0:T(1,128)} %refs_2_.1, s32[1,2]{1,0:T(1,128)} %refs_3_.1, s32[2,256]{1,0:T(2,128)} %bitcast.12, s32[1,2]{1,0:T(1,128)} %bitcast.13, s32[2,1326]{1,0:T(2,128)} %bitcast.9, ...), custom_call_target="tpu_custom_call" | custom-call | tf_op jit(solution)/shard_map/pallas_call | solution.py:308
  48.5 0.0 copy-start
  48.5 1.3 %copy.14 = f32[1,2,1326]{2,1,0:T(2,128)} copy(f32[1,2,1326]{2,1,0:T(2,128)} %bitcast.7) | data formatting | bytes 21216
  49.8 0.0 copy-done
  49.8 0.6 %copy.15 = f32[1,1326]{1,0:T(1,128)} copy(f32[1,1326]{1,0:T(1,128)S(1)} %copy-done) | data formatting | bytes 10608
Async XLA Ops:
  48.5 1.3 %copy-start = (f32[1,1326]{1,0:T(1,128)S(1)}, f32[1,1326]{1,0:T(1,128)}, u32[]{:S(2)}) copy-start(f32[1,1326]{1,0:T(1,128)} %get-tuple-element.9) | copy-start | bytes 15916

commit v4 on v3

--- a/solution.py
+++ b/solution.py
@@ -20,6 +20,7 @@
 FLOOR = 0.1
 N = 8
 PARTS = (0, 128, 192)
+FAR = (4, 3, 5, 2, 6, 1, 7)
 MESH = pl.DeviceIdType.MESH
 BF16 = jnp.bfloat16
 F32 = jnp.float32
@@ -76,11 +77,11 @@
         load.start()
 
     barrier = pltpu.get_barrier_semaphore()
-    for d in range(1, N):
+    for d in FAR:
         pl.semaphore_signal(barrier, inc=1, device_id=on_z(d), device_id_type=MESH)
         pl.semaphore_signal(barrier, inc=1, device_id=on_y(d), device_id_type=MESH)
     pl.semaphore_signal(barrier, inc=1, device_id=other_core, device_id_type=MESH)
-    for d in range(1, 4):
+    for d in (2, 1, 3):
         pl.semaphore_signal(barrier, inc=1, device_id=(lax.rem(f + d, 4), t, z), device_id_type=MESH)
 
     for load in loads:
@@ -117,7 +118,6 @@
             minus_apart[rows, cols] = -free
         return carry
 
-    lax.fori_loop(0, TILES, spread, 0)
 
     def prepare(s):
         for k in range(2):
@@ -163,18 +163,19 @@
         pltpu.make_async_copy(ref, ref, sem).wait()
 
     remote(board.at[0], board.at[1], sem_board.at[0], sem_board.at[1], other_core)
-    for d in range(1, N):
+    for d in FAR:
         remote(line_a.at[z], line_a.at[z], ag_send.at[0], ag_recv.at[0], on_z(d))
         remote(line_b.at[y], line_b.at[y], ag_send.at[1], ag_recv.at[1], on_y(d))
 
+    lax.fori_loop(0, TILES, spread, 0)
     prepare(0)
     arrived(ag_recv.at[0], line_a.at[0 : N - 1])
     rows_a[y] = line_a[...].reshape(16, SPLIT)
-    for d in range(1, N):
+    for d in FAR:
         remote(rows_a.at[y], rows_a.at[y], ag_send.at[2], ag_recv.at[2], on_y(d))
     arrived(ag_recv.at[1], line_b.at[0 : N - 1])
     rows_b[z] = line_b[...].reshape(16, HP - SPLIT)
-    for d in range(1, N):
+    for d in FAR:
         remote(rows_b.at[z], rows_b.at[z], ag_send.at[3], ag_recv.at[3], on_z(d))
 
     generate(0)
@@ -230,7 +231,7 @@
             part_a[m] = total.reshape(N, N, 2, width)
         else:
             part_b[m, :, 0:width] = total
-        for d in range(1, N):
+        for d in FAR:
             if o == 0:
                 src, dst, device = part_a.at[m, :, z_peer(d)], recv_a.at[m, d], on_z(d)
             else:
@@ -249,25 +250,25 @@
         arrived(rs1_recv.at[n], landed(n))
         if o == 0:
             total = part_a[m, :, z]
-            for d in range(1, N):
+            for d in FAR:
                 total += recv_a[m, d]
             mid[:, :, cols] = total
         else:
             total = part_b[m, pl.ds(pl.multiple_of(y * 16, 16), 16), 0:width]
-            for d in range(1, N):
+            for d in FAR:
                 total += recv_b[m, d, :, 0:width]
             for q in range(N):
                 mid[q, :, cols] = total[2 * q : 2 * q + 2]
         if n >= len(CHUNKS) - 2:
             whole = halves[o]
-            for d in range(1, N):
+            for d in FAR:
                 target, device = (y_peer(d), on_y(d)) if o == 0 else (z_peer(d), on_z(d))
                 remote(mid.at[target, :, whole], recv2.at[d, :, whole], rs2_send.at[o], rs2_recv.at[o], device)
     arrived(rs2_recv.at[0], recv2.at[1:N, :, halves[0]])
     arrived(rs2_recv.at[1], recv2.at[1:N, :, halves[1]])
     value_a = mid[y, :, 0:SPLIT]
     value_b = mid[z, :, SPLIT:H]
-    for d in range(1, N):
+    for d in FAR:
         value_a += recv2[d, :, 0:SPLIT]
         value_b += recv2[d, :, SPLIT:H]
     row_id = lax.broadcasted_iota(jnp.int32, (2, LANES), 0)
@@ -283,7 +284,7 @@
         new_regrets[:, first:last] = jnp.maximum(held_regret + worth - decision, 0.0)
         node[f, :, first:last] = decision
 
-    for d in range(1, 4):
+    for d in (2, 1, 3):
         remote(node.at[f], node.at[f], fl_sems.at[0], fl_sems.at[1], (lax.rem(f + d, 4), t, z))
     arrived(fl_sems.at[1], node.at[0:3])
     chance[...] = ((node[0] + node[1]) + (node[2] + node[3])) * 0.25
@@ -357,11 +358,16 @@
             dma((2,)),
         ],
         compiler_params=pltpu.CompilerParams(
-            collective_id=0, has_side_effects=True, vmem_limit_bytes=63 * 1024 * 1024
+            collective_id=0, has_side_effects=True, vmem_limit_bytes=48 * 1024 * 1024
         ),
     )(
-        regrets[0], opp_reach[0], pot_size, line_kind, board_lines[0, 0], board_count[0],
-        hand_ranks[0, 0], live_hands[0, 0], jnp.asarray(left), jnp.asarray(right),
+        *(
+            pltpu.with_memory_space_constraint(array, pltpu.HBM)
+            for array in (
+                regrets[0], opp_reach[0], pot_size, line_kind, board_lines[0, 0], board_count[0],
+                hand_ranks[0, 0], live_hands[0, 0], jnp.asarray(left), jnp.asarray(right),
+            )
+        )
     )
     return updated[None], chance
 

time: 50.6 us -> 46.7 us (0.923)
  Pallas kernels: 47.8 us -> 44.7 us
  local copies, waits for them, and re-layouts: 1.91 us -> 1.19 us
    pallas_call x1, Pallas kernels: 47.8 us -> 44.7 us  [on_device(): pl.pallas_call(kernel, out_shape=(jax.ShapeDtypeStruct((2, H), F32), jax....]
    unnamed x4 -> x2, local copies, waits for them, and re-layouts: 1.91 us -> 1.19 us
where the time goes in v4:
time: 46.7 us; the launch traced here: 46.5 us
  Pallas kernels  44.7 us (96%)
  local copies, waits for them, and re-layouts  1.19 us (3%)
  between operations  0.64 us (1%)
    pallas_call x1, Pallas kernels, on_device(): pl.pallas_call(kernel, out_shape=(jax.ShapeDtypeStruct((2, H), F32), jax....  44.7 us
    unnamed x2, local copies, waits for them, and re-layouts  1.19 us

profile of v4, /device:TPU:2, one launch (start us, length us, event | category | flops | bytes accessed | tf_op | source)
XLA Modules:
  0.0 46.5 jit_solution(13394734330338540605)
XLA Ops:
  0.6 44.7 %shard_map.113 = (f32[2,1326]{1,0:T(2,128)S(1)}, f32[1,1326]{1,0:T(1,128)S(1)}) custom-call(f32[2,1326]{1,0:T(2,128)} %bitcast.8, bf16[2,1326]{1,0:T(2,128)(2,1)} %bitcast.11, s32[1,2]{1,0:T(1,128)} %refs_2_.1, s32[1,2]{1,0:T(1,128)} %refs_3_.1, s32[2,256]{1,0:T(2,128)} %bitcast.12, s32[1,2]{1,0:T(1,128)} %bitcast.13, s32[2,1326]{1,0:T(2,128)} %bitcast.9, ...), custom_call_target="tpu_custom_call" | custom-call | tf_op jit(solution)/shard_map/pallas_call | solution.py:309
  45.3 0.6 %copy.14 = f32[1,2,1326]{2,1,0:T(2,128)} copy(f32[1,2,1326]{2,1,0:T(2,128)S(1)} %bitcast.7) | data formatting | bytes 21216
  45.9 0.6 %copy.15 = f32[1,1326]{1,0:T(1,128)} copy(f32[1,1326]{1,0:T(1,128)S(1)} %get-tuple-element.9) | data formatting | bytes 10608

commit v5 on v4

--- a/solution.py
+++ b/solution.py
@@ -20,7 +20,7 @@
 FLOOR = 0.1
 N = 8
 PARTS = (0, 128, 192)
-FAR = (4, 3, 5, 2, 6, 1, 7)
+FAR = (4, 5, 3, 6, 2, 7, 1)
 MESH = pl.DeviceIdType.MESH
 BF16 = jnp.bfloat16
 F32 = jnp.float32
@@ -168,16 +168,15 @@
         remote(line_b.at[y], line_b.at[y], ag_send.at[1], ag_recv.at[1], on_y(d))
 
     lax.fori_loop(0, TILES, spread, 0)
-    prepare(0)
     arrived(ag_recv.at[0], line_a.at[0 : N - 1])
+    arrived(ag_recv.at[1], line_b.at[0 : N - 1])
     rows_a[y] = line_a[...].reshape(16, SPLIT)
+    rows_b[z] = line_b[...].reshape(16, HP - SPLIT)
     for d in FAR:
         remote(rows_a.at[y], rows_a.at[y], ag_send.at[2], ag_recv.at[2], on_y(d))
-    arrived(ag_recv.at[1], line_b.at[0 : N - 1])
-    rows_b[z] = line_b[...].reshape(16, HP - SPLIT)
-    for d in FAR:
         remote(rows_b.at[z], rows_b.at[z], ag_send.at[3], ag_recv.at[3], on_z(d))
 
+    prepare(0)
     generate(0)
     arrived(sem_board.at[1], board.at[1])
     prepare(1)

time: 46.7 us -> 46.4 us (level)
  the two profiles are of different devices: /device:TPU:2 before, /device:TPU:8 now
where the time goes in v5:
time: 46.4 us; the launch traced here: 46.2 us
  Pallas kernels  44.4 us (96%)
  local copies, waits for them, and re-layouts  1.19 us (3%)
  between operations  0.64 us (1%)
    pallas_call x1, Pallas kernels, on_device(): pl.pallas_call(kernel, out_shape=(jax.ShapeDtypeStruct((2, H), F32), jax....  44.4 us
    unnamed x2, local copies, waits for them, and re-layouts  1.19 us

profile of v5, /device:TPU:8, one launch (start us, length us, event | category | flops | bytes accessed | tf_op | source)
XLA Modules:
  0.0 46.2 jit_solution(16926203188981829735)
XLA Ops:
  0.6 44.4 %shard_map.113 = (f32[2,1326]{1,0:T(2,128)S(1)}, f32[1,1326]{1,0:T(1,128)S(1)}) custom-call(f32[2,1326]{1,0:T(2,128)} %bitcast.8, bf16[2,1326]{1,0:T(2,128)(2,1)} %bitcast.11, s32[1,2]{1,0:T(1,128)} %refs_2_.1, s32[1,2]{1,0:T(1,128)} %refs_3_.1, s32[2,256]{1,0:T(2,128)} %bitcast.12, s32[1,2]{1,0:T(1,128)} %bitcast.13, s32[2,1326]{1,0:T(2,128)} %bitcast.9, ...), custom_call_target="tpu_custom_call" | custom-call | tf_op jit(solution)/shard_map/pallas_call | solution.py:308
  45.0 0.6 %copy.14 = f32[1,2,1326]{2,1,0:T(2,128)} copy(f32[1,2,1326]{2,1,0:T(2,128)S(1)} %bitcast.7) | data formatting | bytes 21216
  45.6 0.6 %copy.15 = f32[1,1326]{1,0:T(1,128)} copy(f32[1,1326]{1,0:T(1,128)S(1)} %get-tuple-element.9) | data formatting | bytes 10608
